TPU v7x, 32 devices: a whole 2x2x4 slice. The times are simulated.
32 devices in a mesh: date: 2 (over y), row: 16 (over z, x, core).
Axes of the slice: x: 2, y: 2, z: 4, core: 2. Of those that a mesh axis runs over, the one named last changes fastest.
Arguments:
- slc: float32 [2, 128, 128, 256], P(None, 'date', 'row'), may hold values from -40 to 40, as said below
- network: int32 [128, 8], replicated, may hold values 0 or 1
Outputs:
- linked: float32 [2, 128, 128, 256], P(None, None, 'row', 'date')
Inputs may be any that keep to these rules, and one draw needn't show every extreme that they name: slc holds real and imaginary parts of complex samples.
All inputs are finite; a program needn't handle non-finite values.
Results may differ from a plain program's by a relative error of at most 0.0003.
Values sent between devices are 32-bit elements; how exact they have to be, the bound alone decides.
A program may use at most 192 MiB of HBM per device.

v0:
```python
import jax
import jax.numpy as jnp
from jax import lax
from jax.sharding import PartitionSpec as P

LOOK = 5
ITERS = 5


def extended_2(cells, sides, width):
    for axis, dim in sides:
        count = lax.axis_size(axis)
        ends = count - 1
        head = lax.slice_in_dim(cells, 0, width, axis=dim)
        tail = lax.slice_in_dim(cells, cells.shape[dim] - width, cells.shape[dim], axis=dim)
        cells = jnp.concatenate(
            [
                lax.ppermute(tail, axis, [(i, (i + 1) % count) for i in range(ends)]),
                cells,
                lax.ppermute(head, axis, [((i + 1) % count, i) for i in range(ends)]),
            ],
            axis=dim,
        )
    return cells


def band_table(count_out):
    count_in = count_out + 2 * LOOK
    outer = jnp.arange(count_out, dtype=jnp.int32)[:, None]
    inner = jnp.arange(count_in, dtype=jnp.int32)[None, :]
    reach = inner - outer
    return ((reach >= 0) & (reach <= 2 * LOOK)).astype(jnp.float32)


def box_sum(samples):
    rows_out = samples.shape[-2] - 2 * LOOK
    cols_out = samples.shape[-1] - 2 * LOOK
    row_table = band_table(rows_out)
    col_table = band_table(cols_out)
    total = jnp.einsum("...rc,kr->...kc", samples, row_table, precision=lax.Precision.HIGHEST)
    return jnp.einsum("...kc,mc->...km", total, col_table, precision=lax.Precision.HIGHEST)


def coherence(extended, network):
    num_dates = extended.shape[1]
    squares = extended[0] * extended[0] + extended[1] * extended[1]
    inverse_root = lax.rsqrt(box_sum(squares) + 1e-06)
    layers = []
    for offset in range(1, network.shape[1] + 1):
        earlier = extended[:, : num_dates - offset]
        later = extended[:, offset:]
        prod_re = earlier[0] * later[0] + earlier[1] * later[1]
        prod_im = earlier[1] * later[0] - earlier[0] * later[1]
        sums = box_sum(jnp.stack([prod_re, prod_im]))
        weight = network[: num_dates - offset, offset - 1].astype(jnp.float32)[:, None, None]
        weight = weight * inverse_root[: num_dates - offset] * inverse_root[offset:]
        layer = sums * weight[None]
        layers.append(jnp.pad(layer, ((0, 0), (0, offset), (0, 0), (0, 0))))
    return jnp.stack(layers)


def apply_matrix(coherent, vector):
    num_dates = vector.shape[1]
    image_re = vector[0]
    image_im = vector[1]
    for offset in range(1, coherent.shape[0] + 1):
        coh_re = coherent[offset - 1, 0]
        coh_im = coherent[offset - 1, 1]
        ahead = jnp.pad(vector[:, offset:], ((0, 0), (0, offset), (0, 0), (0, 0)))
        image_re = image_re + coh_re * ahead[0] - coh_im * ahead[1]
        image_im = image_im + coh_re * ahead[1] + coh_im * ahead[0]
        back_re = coh_re * vector[0] + coh_im * vector[1]
        back_im = coh_re * vector[1] - coh_im * vector[0]
        image_re = image_re + jnp.pad(back_re[: num_dates - offset], ((offset, 0), (0, 0), (0, 0)))
        image_im = image_im + jnp.pad(back_im[: num_dates - offset], ((offset, 0), (0, 0), (0, 0)))
    image = jnp.stack([image_re, image_im])
    meansq = jnp.mean(image[0] * image[0] + image[1] * image[1], axis=0)
    return image * lax.rsqrt(meansq + 1e-06)[None, None]


def power_iterate(coherent):
    start = jnp.stack([jnp.ones_like(coherent[0, 0]), jnp.zeros_like(coherent[0, 0])])

    def iterate_once(index, vector):
        return apply_matrix(coherent, vector)

    return lax.fori_loop(0, ITERS, iterate_once, start)


def regroup(samples):
    return lax.all_to_all(samples, "date", split_axis=3, concat_axis=1, tiled=True)


def add_row_rims(samples):
    return extended_2(samples, (("row", 2),), LOOK)


def add_column_rims(samples):
    return extended_2(samples, (("date", 3),), LOOK)


def on_device(slc, network):
    extended = add_column_rims(regroup(add_row_rims(slc)))
    coherent = coherence(extended, network)
    return power_iterate(coherent)


def solution(mesh):
    return jax.shard_map(
        on_device,
        mesh=mesh,
        in_specs=(P(None, "date", "row", None), P()),
        out_specs=P(None, None, "row", "date"),
        check_vma=False,
    )
```

profile of v0, /device:TPU:10, one launch (start us, length us, event | category | flops | bytes accessed | tf_op | source)
XLA Modules:
  0.0 409.5 jit_solution(18203681720282301117)
XLA Ops:
  10.9 11.1 %collective-permute-done = f32[2,64,5,256]{3,1,2,0:T(8,128)} collective-permute-done((f32[2,64,5,256]{3,1,2,0:T(8,128)}, f32[2,64,5,256]{3,1,2,0:T(8,128)}, u32[]{:S(2)}, u32[]{:S(2)}) %collective-permute-start) | collective-permute-done | bytes 655392 | tf_op jit(solution)/shard_map/ppermute | solution.py:18
  29.2 6.1 %fusion.153 = f32[256,2,18,64]{3,2,1,0:T(8,128)} fusion(f32[2,64,5,256]{1,2,0,3:T(8,128)} %copy.74, f32[2,64,8,256]{1,2,0,3:T(8,128)S(1)} %copy.73, f32[2,64,5,256]{1,2,0,3:T(8,128)} %copy.72), kind=kLoop, calls=%fused_computation.235 | loop fusion | flops 1179648 | bytes 4718592
  35.2 6.0 %reshape.70 = f32[2,1,294912]{2,1,0:T(1,128)} reshape(f32[256,2,18,64]{3,2,1,0:T(8,128)} %fusion.153) | data formatting | bytes 4718592
  45.6 23.0 %all-to-all-done = f32[2,1,294912]{2,1,0:T(1,128)S(1)} async-done(((f32[2,1,294912]{2,1,0:T(1,128)}), f32[2,1,294912]{2,1,0:T(1,128)S(1)}, u32[]{:S(2)}, u32[]{:S(2)}) %all-to-all-start) | async-done | bytes 2359328 | tf_op jit(solution)/shard_map/all_to_all | solution.py:91
  69.1 9.0 %reduce = f32[2,294912]{1,0:T(2,128)} reduce(f32[2,1,294912]{2,1,0:T(1,128)S(1)} %all-to-all-done, f32[]{:T(128)} %broadcast.224), dimensions={1}, to_apply=%all_to_all.13.reduce_sub_computation | reduce | bytes 4718596 | tf_op jit(solution)/shard_map/all_to_all | solution.py:91
  78.1 7.5 %reshape.71 = f32[256,2,18,64]{3,2,1,0:T(8,128)} reshape(f32[2,294912]{1,0:T(2,128)} %reduce) | data formatting | bytes 4718592
  85.7 6.4 %copy.100 = f32[2,64,18,2,128]{4,3,1,2,0:T(2,128)} copy(f32[2,64,18,2,128]{1,2,0,4,3:T(8,128)} %bitcast.423) | data formatting | bytes 4718592 | tf_op jit(solution)/shard_map/all_to_all | solution.py:91
  113.2 5.5 %multiply_add_fusion.9 = (f32[1,121,18,138]{1,0,3,2:T(1,128)S(1)}, f32[1,121,18,138]{1,0,3,2:T(1,128)S(1)}) fusion(f32[2,128,18,138]{1,0,3,2:T(2,128)S(1)} %pad_maximum_fusion.1), kind=kLoop, calls=%fused_computation.114 | loop fusion | flops 1803384 | bytes 7213536 | tf_op jit(solution)/shard_map/add | solution.py:52
  121.5 6.4 %multiply_add_fusion.8 = (f32[1,120,18,138]{1,0,3,2:T(1,128)}, f32[1,120,18,138]{1,0,3,2:T(1,128)}) fusion(f32[2,128,18,138]{1,0,3,2:T(2,128)S(1)} %pad_maximum_fusion.1), kind=kLoop, calls=%fused_computation.112 | loop fusion | flops 1788480 | bytes 7153920 | tf_op jit(solution)/shard_map/add | solution.py:52
  127.8 6.4 %multiply_add_fusion.11 = (f32[1,123,18,138]{1,0,3,2:T(1,128)}, f32[1,123,18,138]{1,0,3,2:T(1,128)}) fusion(f32[2,128,18,138]{1,0,3,2:T(2,128)S(1)} %pad_maximum_fusion.1), kind=kLoop, calls=%fused_computation.118 | loop fusion | flops 1833192 | bytes 7332768 | tf_op jit(solution)/shard_map/add | solution.py:52
  134.2 6.4 %multiply_add_fusion.10 = (f32[1,122,18,138]{1,0,3,2:T(1,128)}, f32[1,122,18,138]{1,0,3,2:T(1,128)}) fusion(f32[2,128,18,138]{1,0,3,2:T(2,128)S(1)} %pad_maximum_fusion.1), kind=kLoop, calls=%fused_computation.116 | loop fusion | flops 1818288 | bytes 7273152 | tf_op jit(solution)/shard_map/add | solution.py:52
  140.6 6.6 %multiply_add_fusion.13 = (f32[1,125,18,138]{1,0,3,2:T(1,128)}, f32[1,125,18,138]{1,0,3,2:T(1,128)}) fusion(f32[2,128,18,138]{1,0,3,2:T(2,128)S(1)} %pad_maximum_fusion.1), kind=kLoop, calls=%fused_computation.122 | loop fusion | flops 1863000 | bytes 7452000 | tf_op jit(solution)/shard_map/add | solution.py:52
  147.2 6.4 %multiply_add_fusion.12 = (f32[1,124,18,138]{1,0,3,2:T(1,128)}, f32[1,124,18,138]{1,0,3,2:T(1,128)}) fusion(f32[2,128,18,138]{1,0,3,2:T(2,128)S(1)} %pad_maximum_fusion.1), kind=kLoop, calls=%fused_computation.120 | loop fusion | flops 1848096 | bytes 7392384 | tf_op jit(solution)/shard_map/add | solution.py:52
  153.6 6.5 %multiply_add_fusion.15 = (f32[1,127,18,138]{1,0,3,2:T(1,128)}, f32[1,127,18,138]{1,0,3,2:T(1,128)}) fusion(f32[2,128,18,138]{1,0,3,2:T(2,128)S(1)} %pad_maximum_fusion.1), kind=kLoop, calls=%fused_computation.126 | loop fusion | flops 1892808 | bytes 7571232 | tf_op jit(solution)/shard_map/add | solution.py:52
  160.1 6.4 %multiply_add_fusion.14 = (f32[1,126,18,138]{1,0,3,2:T(1,128)}, f32[1,126,18,138]{1,0,3,2:T(1,128)}) fusion(f32[2,128,18,138]{1,0,3,2:T(2,128)S(1)} %pad_maximum_fusion.1), kind=kLoop, calls=%fused_computation.124 | loop fusion | flops 1877904 | bytes 7511616 | tf_op jit(solution)/shard_map/add | solution.py:52
  169.3 6.7 %copy.94 = f32[2,121,18,138]{3,2,1,0:T(8,128)} copy(f32[2,121,18,138]{1,0,3,2:T(2,128)S(1)} %pad_maximum_fusion.8) | data formatting | bytes 4809024 | tf_op jit(solution)/shard_map/stack | solution.py:54
  176.0 6.2 %fusion.91 = f32[8,2,121,138]{3,0,2,1:T(8,128)} fusion(f32[2,121,18,138]{3,2,1,0:T(8,128)} %copy.94), kind=kOutput, calls=%fused_computation.174 | convolution fusion | flops 57708864 | bytes 3473184 | tf_op jit(solution)/shard_map/...rc,kr->...kc/dot_general | solution.py:40
  188.1 6.3 %copy.96 = f32[2,120,18,138]{3,2,1,0:T(8,128)} copy(f32[2,120,18,138]{1,0,3,2:T(2,128)S(1)} %pad_maximum_fusion.9) | data formatting | bytes 4769280 | tf_op jit(solution)/shard_map/stack | solution.py:54
  194.4 6.1 %fusion.89 = f32[8,2,120,138]{3,0,2,1:T(8,128)} fusion(f32[2,120,18,138]{3,2,1,0:T(8,128)} %copy.96), kind=kOutput, calls=%fused_computation.172 | convolution fusion | flops 57231936 | bytes 3444480 | tf_op jit(solution)/shard_map/...rc,kr->...kc/dot_general | solution.py:40
  204.7 6.3 %copy.90 = f32[2,123,18,138]{3,2,1,0:T(8,128)} copy(f32[2,123,18,138]{1,0,3,2:T(2,128)S(1)} %pad_maximum_fusion.6) | data formatting | bytes 4888512 | tf_op jit(solution)/shard_map/stack | solution.py:54
  211.0 6.1 %fusion.95 = f32[8,2,123,138]{3,0,2,1:T(8,128)} fusion(f32[2,123,18,138]{3,2,1,0:T(8,128)} %copy.90), kind=kOutput, calls=%fused_computation.178 | convolution fusion | flops 58662720 | bytes 3530592 | tf_op jit(solution)/shard_map/...rc,kr->...kc/dot_general | solution.py:40
  221.8 6.5 %copy.92 = f32[2,122,18,138]{3,2,1,0:T(8,128)} copy(f32[2,122,18,138]{1,0,3,2:T(2,128)S(1)} %pad_maximum_fusion.7) | data formatting | bytes 4848768 | tf_op jit(solution)/shard_map/stack | solution.py:54
  228.3 6.0 %fusion.93 = f32[8,2,122,138]{3,0,2,1:T(8,128)} fusion(f32[2,122,18,138]{3,2,1,0:T(8,128)} %copy.92), kind=kOutput, calls=%fused_computation.176 | convolution fusion | flops 58185792 | bytes 3501888 | tf_op jit(solution)/shard_map/...rc,kr->...kc/dot_general | solution.py:40
  239.0 6.3 %copy.86 = f32[2,125,18,138]{3,2,1,0:T(8,128)} copy(f32[2,125,18,138]{1,0,3,2:T(2,128)S(1)} %pad_maximum_fusion.4) | data formatting | bytes 4968000 | tf_op jit(solution)/shard_map/stack | solution.py:54
  245.3 6.2 %fusion.99 = f32[8,2,125,138]{3,0,2,1:T(8,128)} fusion(f32[2,125,18,138]{3,2,1,0:T(8,128)} %copy.86), kind=kOutput, calls=%fused_computation.182 | convolution fusion | flops 59616576 | bytes 3588000 | tf_op jit(solution)/shard_map/...rc,kr->...kc/dot_general | solution.py:40
  256.2 6.8 %copy.88 = f32[2,124,18,138]{3,2,1,0:T(8,128)} copy(f32[2,124,18,138]{1,0,3,2:T(2,128)S(1)} %pad_maximum_fusion.5) | data formatting | bytes 4928256 | tf_op jit(solution)/shard_map/stack | solution.py:54
  263.0 6.2 %fusion.97 = f32[8,2,124,138]{3,0,2,1:T(8,128)} fusion(f32[2,124,18,138]{3,2,1,0:T(8,128)} %copy.88), kind=kOutput, calls=%fused_computation.180 | convolution fusion | flops 59139648 | bytes 3559296 | tf_op jit(solution)/shard_map/...rc,kr->...kc/dot_general | solution.py:40
  273.9 6.3 %copy.80 = f32[2,127,18,138]{3,2,1,0:T(8,128)} copy(f32[2,127,18,138]{1,0,3,2:T(2,128)S(1)} %pad_maximum_fusion.2) | data formatting | bytes 5047488 | tf_op jit(solution)/shard_map/stack | solution.py:54
  280.2 6.3 %fusion.103 = f32[8,2,127,138]{3,0,2,1:T(8,128)} fusion(f32[2,127,18,138]{3,2,1,0:T(8,128)} %copy.80), kind=kOutput, calls=%fused_computation.186 | convolution fusion | flops 60570432 | bytes 3645408 | tf_op jit(solution)/shard_map/...rc,kr->...kc/dot_general | solution.py:40
  291.3 6.5 %copy.84 = f32[2,126,18,138]{3,2,1,0:T(8,128)} copy(f32[2,126,18,138]{1,0,3,2:T(2,128)S(1)} %pad_maximum_fusion.3) | data formatting | bytes 5007744 | tf_op jit(solution)/shard_map/stack | solution.py:54
  297.7 4.9 %fusion.101 = f32[8,2,126,138]{3,0,2,1:T(8,128)S(1)} fusion(f32[2,126,18,138]{3,2,1,0:T(8,128)} %copy.84), kind=kOutput, calls=%fused_computation.184 | convolution fusion | flops 60093504 | bytes 3616704 | tf_op jit(solution)/shard_map/...rc,kr->...kc/dot_general | solution.py:40
  322.6 85.7 %while.12 = (s32[]{:T(128)}, f32[2,128,8,128]{3,2,1,0:T(8,128)S(1)}, f32[1,2,128,8,128]{4,3,2,1,0:T(8,128)}, f32[1,2,128,8,128]{4,3,2,1,0:T(8,128)}, f32[1,2,128...) while((s32[]{:T(128)}, ...), condition=%wide.region_2.3_spmd, body=%wide.region_0.2_spmd.sunk | while | flops 17605632 | bytes 115360056 | solution.py:87
  (325 shorter events, 188.7 us)
Async XLA Ops:
  1.7 7.7 %copy-start.8 = (f32[2,64,8,256]{3,2,1,0:T(8,128)S(1)}, f32[2,64,8,256]{3,2,1,0:T(8,128)}, u32[]{:S(2)}) copy-start(f32[2,64,8,256]{3,2,1,0:T(8,128)} %param.4) | copy-start | bytes 3145732
  2.8 19.2 %collective-permute-start = (f32[2,64,5,256]{3,1,2,0:T(8,128)}, f32[2,64,5,256]{3,1,2,0:T(8,128)}, u32[]{:S(2)}, u32[]{:S(2)}) collective-permute-start(f32[2,64,5,256]{3,1,2,0:T(8,128)} %copy.102), channel_id=1, source_target_pairs={{0,1},{1,2},{2,3},{3,4},{4,5},{5,6},{6,7},{7,8},{8,9},{9,10},{10,1... | collective-permute-start | bytes 1966088 | tf_op jit(solution)/shard_map/ppermute | solution.py:18
  4.7 6.2 %copy-start.39 = (s32[128,8]{0,1:T(8,128)S(1)}, s32[128,8]{0,1:T(8,128)}, u32[]{:S(2)}) copy-start(s32[128,8]{0,1:T(8,128)} %param.5) | copy-start | bytes 12292
  5.8 19.9 %collective-permute-start.1 = (f32[2,64,5,256]{3,1,2,0:T(8,128)}, f32[2,64,5,256]{3,1,2,0:T(8,128)}, u32[]{:S(2)}, u32[]{:S(2)}) collective-permute-start(f32[2,64,5,256]{3,1,2,0:T(8,128)} %copy.103), channel_id=1, source_target_pairs={{1,0},{2,1},{3,2},{4,3},{5,4},{6,5},{7,6},{8,7},{9,8},{10,9},{11,1... | collective-permute-start | bytes 1966088 | tf_op jit(solution)/shard_map/ppermute | solution.py:20
  41.2 27.4 %all-to-all-start = ((f32[2,1,294912]{2,1,0:T(1,128)}), f32[2,1,294912]{2,1,0:T(1,128)S(1)}, u32[]{:S(2)}, u32[]{:S(2)}) async-start(f32[2,1,294912]{2,1,0:T(1,128)} %reshape.70), calls=%async_computation | async-start | bytes 4718592 | tf_op jit(solution)/shard_map/all_to_all | solution.py:91
  99.4 9.1 %collective-permute-start.2 = (f32[2,128,18,5]{1,0,3,2:T(2,128)S(1)}, f32[2,128,18,5]{1,0,3,2:T(2,128)S(1)}, u32[]{:S(2)}, u32[]{:S(2)}) collective-permute-start(f32[2,128,18,5]{1,0,3,2:T(2,128)S(1)} %copy.77), channel_id=1, source_target_pairs={{0,16},{1,17},{2,18},{3,19},{4,20},{5,21},{6,22},{7,23},{8,24},{9,... | collective-permute-start | bytes 276488 | tf_op jit(solution)/shard_map/ppermute | solution.py:18
  104.0 6.4 %collective-permute-start.3 = (f32[2,128,18,5]{1,0,3,2:T(2,128)S(1)}, f32[2,128,18,5]{1,0,3,2:T(2,128)S(1)}, u32[]{:S(2)}, u32[]{:S(2)}) collective-permute-start(f32[2,128,18,5]{1,0,3,2:T(2,128)S(1)} %copy.78), channel_id=1, source_target_pairs={{16,0},{17,1},{18,2},{19,3},{20,4},{21,5},{22,6},{23,7},{24,8},{25... | collective-permute-start | bytes 276488 | tf_op jit(solution)/shard_map/ppermute | solution.py:20
  176.0 6.2 %copy-start.16 = (f32[1,128,18,138]{1,0,3,2:T(1,128)S(1)}, f32[1,128,18,138]{1,0,3,2:T(1,128)}, u32[]{:S(2)}) copy-start(f32[1,128,18,138]{1,0,3,2:T(1,128)} %fusion.59) | copy-start | bytes 3815428
  182.9 2.3 copy-start.29
  182.9 2.3 copy-start.30
  194.3 7.0 %copy-start.28 = (f32[1,123,18,138]{1,0,3,2:T(1,128)S(1)}, f32[1,123,18,138]{1,0,3,2:T(1,128)}, u32[]{:S(2)}) copy-start(f32[1,123,18,138]{1,0,3,2:T(1,128)} %get-tuple-element.203) | copy-start | bytes 3666388
  217.1 1.9 copy-start.26
  234.3 1.9 copy-start.24
  251.5 1.9 copy-start.22
  269.2 1.9 copy-start.20
  286.6 1.9 copy-start.18
  302.8 2.6 copy-start.15
  302.8 2.6 copy-start.37
  310.9 2.3 copy-start.10
  310.9 2.4 copy-start.32
  316.1 2.3 copy-start.9
  316.1 2.4 copy-start.31
  324.4 1.9 copy-start.4
  327.6 1.9 copy-start.2
  341.6 1.9 copy-start.4
  344.7 1.9 copy-start.2
  358.7 1.9 copy-start.4
  361.9 1.9 copy-start.2
  375.8 1.9 copy-start.4
  379.0 1.9 copy-start.2
  393.0 1.9 copy-start.4
  396.1 1.9 copy-start.2
  (41 other events, 58.2 us)
where the time goes:
time: 416 us; the launch traced here: 409 us
  other arithmetic  154 us (37%)
  local copies, waits for them, and re-layouts  145 us (35%)
  matrix products  58.9 us (14%)
  waiting for transfers between devices  36 us (9%)
  starting transfers between devices  13.6 us (3%)
    another operation x8, local copies, waits for them, and re-layouts, coherence(): sums = box_sum(jnp.stack([prod_re, prod_im]))  51.5 us
    add x8, other arithmetic, coherence(): prod_re = earlier[0] * later[0] + earlier[1] * later[1]  50.5 us
    dot_general x9, matrix products, box_sum(): jnp.einsum('...rc,kr->...kc', samples, row_table, precision=lax.Precision...  48.7 us
    sub x40, other arithmetic, apply_matrix(): back_im = coh_re * vector[1] - coh_im * vector[0]  39 us
    unnamed x71, local copies, waits for them, and re-layouts  27.1 us
    all_to_all x1, waiting for transfers between devices, regroup(): lax.all_to_all(samples, 'date', split_axis=3, concat_axis=1, tiled=True)  23 us
    another operation x8, other arithmetic, coherence(): sums = box_sum(jnp.stack([prod_re, prod_im]))  22.7 us
    reduce_sum x5, other arithmetic, apply_matrix(): meansq = jnp.mean(image[0] * image[0] + image[1] * image[1], axis=0)  20.3 us
  transfers between devices with their start and end apart: 5, of which 3 were waited for; matrix products, arithmetic and copies ran while one was open for 3% of the time, Pallas kernels for 0%

commit v1 on v0

v1 whole, which is shorter than its diff:
```python
import functools

import jax
import jax.numpy as jnp
from jax import lax
from jax.experimental import pallas as pl
from jax.experimental.pallas import tpu as pltpu
from jax.sharding import PartitionSpec as P

LOOK = 5
ITERS = 5
SUB = 8
MESH = pl.DeviceIdType.MESH


def pack_kernel(nd, x_ref, s_ref):
    _, dates, rows, cols = x_ref.shape
    width = cols // nd
    groups = dates // SUB
    slot = width // groups
    lane = lax.broadcasted_iota(jnp.int32, (rows, SUB, width), 2)
    for comp in range(2):
        rims = [jnp.zeros((rows, SUB, width), jnp.float32) for _ in range(nd)]
        for g in range(groups):
            near = pl.ds(g * SUB, SUB)
            tiles = []
            for c in range(nd):
                tile = x_ref[comp, near, :, pl.ds(c * width, width)]
                tile = jnp.transpose(tile, (1, 0, 2))
                s_ref[c, comp, :, near, :] = tile
                tiles.append(tile)
            first = slot * g
            for c in range(nd):
                if c > 0:
                    moved = pltpu.roll(tiles[c - 1], (first + LOOK) % width, 2)
                    rims[c] = jnp.where((lane >= first) & (lane < first + LOOK), moved, rims[c])
                if c < nd - 1:
                    moved = pltpu.roll(tiles[c + 1], (first + LOOK) % width, 2)
                    rims[c] = jnp.where((lane >= first + LOOK) & (lane < first + 2 * LOOK), moved, rims[c])
        for c in range(nd):
            s_ref[c, comp, :, pl.ds(dates, SUB), :] = rims[c]


def send_kernel(nd, nr, s_ref, e_ref, give_sem, take_sem, up_send, up_recv, down_send, down_recv):
    rows = s_ref.shape[2]
    me = lax.axis_index("date")
    row = lax.axis_index("row")
    has_up = row > 0
    has_down = row < nr - 1
    up = jnp.maximum(row - 1, 0)
    down = jnp.minimum(row + 1, nr - 1)
    barrier = pltpu.get_barrier_semaphore()
    for k in range(1, nd):
        pl.semaphore_signal(barrier, 1, device_id=(lax.rem(me + k, nd), row), device_id_type=MESH)

    @pl.when(has_up)
    def _():
        pl.semaphore_signal(barrier, 1, device_id=(me, up), device_id_type=MESH)

    @pl.when(has_down)
    def _():
        pl.semaphore_signal(barrier, 1, device_id=(me, down), device_id_type=MESH)

    pl.semaphore_wait(barrier, nd - 1 + has_up.astype(jnp.int32) + has_down.astype(jnp.int32))

    def give(k, comp):
        there = lax.rem(me + k, nd)
        return pltpu.make_async_remote_copy(
            src_ref=s_ref.at[there, comp],
            dst_ref=e_ref.at[me, comp, pl.ds(LOOK, rows)],
            send_sem=give_sem.at[k, comp],
            recv_sem=take_sem.at[k, comp],
            device_id=(there, row),
            device_id_type=MESH,
        )

    def rim(k, comp, to_up):
        source = lax.rem(me + nd - k, nd)
        begin = 0 if to_up else rows - LOOK
        if k == 0:
            src = s_ref.at[me, comp, pl.ds(begin, LOOK)]
        else:
            src = e_ref.at[source, comp, pl.ds(LOOK + begin, LOOK)]
        return pltpu.make_async_remote_copy(
            src_ref=src,
            dst_ref=e_ref.at[source, comp, pl.ds(LOOK + rows if to_up else 0, LOOK)],
            send_sem=(up_send if to_up else down_send).at[k, comp],
            recv_sem=(up_recv if to_up else down_recv).at[k, comp],
            device_id=(me, up if to_up else down),
            device_id_type=MESH,
        )

    def start_rims(k, comp):
        @pl.when(has_up)
        def _():
            rim(k, comp, True).start()

        @pl.when(has_down)
        def _():
            rim(k, comp, False).start()

    for comp in range(2):
        for k in range(1, nd):
            give(k, comp).start()
        start_rims(0, comp)
    for comp in range(2):
        for k in range(1, nd):
            give(k, comp).wait_recv()
            start_rims(k, comp)
    for comp in range(2):
        for k in range(1, nd):
            give(k, comp).wait_send()
    for comp in range(2):
        for k in range(nd):

            @pl.when(has_up)
            def _():
                rim(k, comp, True).wait_send()
                rim(k, comp, False).wait_recv()

            @pl.when(has_down)
            def _():
                rim(k, comp, False).wait_send()
                rim(k, comp, True).wait_recv()


def row_sums(cells):
    span = 2 * LOOK + 1
    count = len(cells) - span + 1
    head = functools.reduce(jnp.add, cells[count - 1 : span])
    heads = [head]
    for k in range(count - 2, -1, -1):
        heads.append(heads[-1] + cells[k])
    heads = heads[::-1]
    sums = [heads[0]]
    tail = None
    for k in range(1, count):
        cell = cells[span + k - 1]
        tail = cell if tail is None else tail + cell
        sums.append(heads[k] + tail)
    return sums


def halves(sums):
    stacked = jnp.concatenate(sums, axis=0)
    high = stacked.astype(jnp.bfloat16)
    low = (stacked - high.astype(jnp.float32)).astype(jnp.bfloat16)
    return high, low


def products(load, offset):
    depth = load.rows
    if offset == 0:
        squares = []
        for r in range(depth):
            re, im = load(0, r, 0), load(1, r, 0)
            squares.append(re * re + im * im)
        return row_sums(squares)
    part_re, part_im = [], []
    for r in range(depth):
        a_re, a_im = load(0, r, 0), load(1, r, 0)
        b_re, b_im = load(0, r, offset), load(1, r, offset)
        part_re.append(a_re * b_re + a_im * b_im)
        part_im.append(a_im * b_re - a_re * b_im)
    return row_sums(part_re) + row_sums(part_im)


class Loader:
    def __init__(self, read, rows):
        self.read = read
        self.rows = rows

    def __call__(self, comp, row, offset):
        return self.read(comp, row, offset)


def link_kernel(nd, nr, s_ref, e_ref, net_ref, out_ref, main, rim, rim_high, rim_low, table, root, gam, vec):
    rows, width = out_ref.shape[2], out_ref.shape[3]
    dates = out_ref.shape[1]
    band = net_ref.shape[1]
    local = dates // nd
    groups = local // SUB
    slot = width // groups
    tiles = dates // SUB
    tall = rows + 2 * LOOK
    me = lax.axis_index("date")
    row = lax.axis_index("row")
    has_up = row > 0
    has_down = row < nr - 1

    lane = lax.broadcasted_iota(jnp.int32, (SUB, width), 1)
    for comp in range(2):
        for r in range(tall):
            inner = LOOK <= r < LOOK + rows
            keep = None if inner else (has_up if r < LOOK else has_down)
            for s in range(nd):
                block = e_ref[s, comp, r, pl.ds(0, local), :]
                edge = e_ref[s, comp, r, pl.ds(local, SUB), :]
                if keep is not None:
                    block = jnp.where(keep, block, 0.0)
                    edge = jnp.where(keep, edge, 0.0)
                main[comp, r, pl.ds(s * local, local), :] = block
                rim[s, comp, r, pl.ds(0, SUB), :] = edge
            if inner:
                main[comp, r, pl.ds(pl.multiple_of(me * local, SUB), local), :] = s_ref[me, comp, r - LOOK, pl.ds(0, local), :]
                rim[me, comp, r, pl.ds(0, SUB), :] = s_ref[me, comp, r - LOOK, pl.ds(local, SUB), :]
            main[comp, r, pl.ds(dates, SUB), :] = jnp.zeros((SUB, width), jnp.float32)
            for s in range(nd):
                later = pltpu.roll(rim[s, comp, r, pl.ds(0, SUB), :], width - slot, 1)
                if s + 1 < nd:
                    last = pltpu.roll(rim[s + 1, comp, r, pl.ds(0, SUB), :], slot * (groups - 1), 1)
                else:
                    last = jnp.zeros((SUB, width), jnp.float32)
                rim[s, comp, r, pl.ds(SUB, SUB), :] = jnp.where(lane >= slot * (groups - 1), last, later)

    inner = lax.broadcasted_iota(jnp.int32, (width, width), 0)
    outer = lax.broadcasted_iota(jnp.int32, (width, width), 1)
    for g in range(groups):
        table[g, pl.ds(0, width), :] = (jnp.abs(inner - outer) <= LOOK).astype(jnp.float32).astype(jnp.bfloat16)
        cell = inner - slot * g
        left = (cell >= 0) & (cell < LOOK) & (outer <= cell)
        right = (cell >= LOOK) & (cell < 2 * LOOK) & (outer >= width + cell - 2 * LOOK)
        table[g, pl.ds(width, width), :] = (left | right).astype(jnp.float32).astype(jnp.bfloat16)

    def rim_sums(s, carry):
        load = Loader(lambda comp, r, off: rim[s, comp, r, pl.ds(off, SUB), :], tall)
        begin = 0
        for offset in range(band + 1):
            high, low = halves(products(load, offset))
            rim_high[s, pl.ds(begin, high.shape[0]), :] = high
            rim_low[s, pl.ds(begin, high.shape[0]), :] = low
            begin += high.shape[0]
        return carry

    lax.fori_loop(0, nd, rim_sums, 0)

    for k in range(rows):
        root[k, pl.ds(dates, SUB), :] = jnp.zeros((SUB, width), jnp.float32)

    def tile_sums(index, carry):
        t = tiles - 1 - index
        s, g = t // groups, lax.rem(t, groups)
        base = t * SUB
        load = Loader(lambda comp, r, off: main[comp, r, pl.ds(base + off, SUB), :], tall)
        used = net_ref[pl.ds(base, SUB), :].astype(jnp.float32)
        begin = 0
        for offset in range(band + 1):
            high, low = halves(products(load, offset))
            count = high.shape[0]
            high = jnp.concatenate([high, rim_high[s, pl.ds(begin, count), :]], axis=1)
            low = jnp.concatenate([low, rim_low[s, pl.ds(begin, count), :]], axis=1)
            begin += count
            sums = jnp.dot(jnp.concatenate([high, low], axis=0), table[g], preferred_element_type=jnp.float32)
            sums = sums[:count] + sums[count:]
            for k in range(rows):
                if offset == 0:
                    root[k, pl.ds(base, SUB), :] = lax.rsqrt(sums[k * SUB : (k + 1) * SUB] + 1e-06)
                else:
                    weight = root[k, pl.ds(base, SUB), :] * root[k, pl.ds(base + offset, SUB), :]
                    weight = weight * used[:, offset - 1 : offset]
                    at = pl.ds(base * rows + k, SUB, stride=rows)
                    gam[0, offset - 1, at, :] = sums[k * SUB : (k + 1) * SUB] * weight
                    gam[1, offset - 1, at, :] = sums[(rows + k) * SUB : (rows + k + 1) * SUB] * weight
        return carry

    lax.fori_loop(0, tiles, tile_sums, 0)

    zero = jnp.zeros((rows, width), jnp.float32)
    for buf in range(2):
        for comp in range(2):
            for d in range(band):
                vec[buf, comp, dates + d] = zero

    def fill(d, carry):
        vec[0, 0, d] = zero + 1.0
        vec[0, 1, d] = zero
        return carry

    lax.fori_loop(0, dates, fill, 0)

    def iterate(step, scale):
        now = lax.rem(step, 2)
        after = 1 - now

        def block(b, carry):
            acc, near, total = carry
            acc_re, acc_im = [list(a) for a in acc]
            v_re, v_im = [list(a) for a in near]
            for j in range(SUB):
                d = b * SUB + j
                v_re.append(vec[now, 0, d + band])
                v_im.append(vec[now, 1, d + band])
                y_re = acc_re[j] + v_re[j]
                y_im = acc_im[j] + v_im[j]
                at = pl.ds(pl.multiple_of(d * rows, rows), rows)
                for o in range(1, band + 1):
                    c_re = gam[0, o - 1, at, :]
                    c_im = gam[1, o - 1, at, :]
                    y_re = y_re + (c_re * v_re[j + o] - c_im * v_im[j + o])
                    y_im = y_im + (c_re * v_im[j + o] + c_im * v_re[j + o])
                    back_re = c_re * v_re[j] + c_im * v_im[j]
                    back_im = c_re * v_im[j] - c_im * v_re[j]
                    if o == band:
                        acc_re.append(back_re)
                        acc_im.append(back_im)
                    else:
                        acc_re[j + o] = acc_re[j + o] + back_re
                        acc_im[j + o] = acc_im[j + o] + back_im
                vec[after, 0, d] = y_re
                vec[after, 1, d] = y_im
                total = total + (y_re * y_re + y_im * y_im)
            acc = tuple(acc_re[SUB:]), tuple(acc_im[SUB:])
            near = tuple(v_re[SUB:]), tuple(v_im[SUB:])
            return acc, near, total

        none = tuple(zero for _ in range(band))
        near = tuple(tuple(vec[now, comp, d] for d in range(band)) for comp in range(2))
        _, _, total = lax.fori_loop(0, tiles, block, ((none, none), near, zero))
        return scale * lax.rsqrt(scale * scale * (total / dates) + 1e-06)

    scale = lax.fori_loop(0, ITERS, iterate, zero + 1.0)
    final = ITERS % 2

    def finish(d, carry):
        out_ref[0, d] = vec[final, 0, d] * scale
        out_ref[1, d] = vec[final, 1, d] * scale
        return carry

    lax.fori_loop(0, dates, finish, 0)


def on_device(nd, nr, slc, network):
    _, local, rows, cols = slc.shape
    width = cols // nd
    dates, band = network.shape
    tall = rows + 2 * LOOK
    maps = (2 * band + 1) * rows * SUB
    whole = pl.BlockSpec(memory_space=pltpu.VMEM)
    away = pl.BlockSpec(memory_space=pl.ANY)
    packed = pl.pallas_call(
        functools.partial(pack_kernel, nd),
        out_shape=jax.ShapeDtypeStruct((nd, 2, rows, local + SUB, width), jnp.float32),
        in_specs=[whole],
        out_specs=whole,
        name="pack",
    )(slc)
    sems = pltpu.SemaphoreType.DMA((nd, 2))
    landed = pl.pallas_call(
        functools.partial(send_kernel, nd, nr),
        out_shape=jax.ShapeDtypeStruct((nd, 2, tall, local + SUB, width), jnp.float32),
        in_specs=[away],
        out_specs=away,
        scratch_shapes=[sems] * 6,
        compiler_params=pltpu.CompilerParams(collective_id=0, has_side_effects=True),
        name="send",
    )(packed)
    return pl.pallas_call(
        functools.partial(link_kernel, nd, nr),
        out_shape=jax.ShapeDtypeStruct((2, dates, rows, width), jnp.float32),
        in_specs=[whole] * 3,
        out_specs=whole,
        scratch_shapes=[
            pltpu.VMEM((2, tall, dates + SUB, width), jnp.float32),
            pltpu.VMEM((nd, 2, tall, 2 * SUB, width), jnp.float32),
            pltpu.VMEM((nd, maps, width), jnp.bfloat16),
            pltpu.VMEM((nd, maps, width), jnp.bfloat16),
            pltpu.VMEM((local // SUB, 2 * width, width), jnp.bfloat16),
            pltpu.VMEM((rows, dates + SUB, width), jnp.float32),
            pltpu.VMEM((2, band, dates * rows, width), jnp.float32),
            pltpu.VMEM((2, 2, dates + band, rows, width), jnp.float32),
        ],
        compiler_params=pltpu.CompilerParams(vmem_limit_bytes=48 * 1024 * 1024),
        name="link",
    )(packed, landed, network)


def solution(mesh):
    return jax.shard_map(
        functools.partial(on_device, mesh.shape["date"], mesh.shape["row"]),
        mesh=mesh,
        in_specs=(P(None, "date", "row", None), P()),
        out_specs=P(None, None, "row", "date"),
        check_vma=False,
    )
```

time: 416 us -> 52.6 us (0.13)
  the two profiles are of different devices: /device:TPU:10 before, /device:TPU:1 now
where the time goes in v1:
time: 52.6 us; the launch traced here: 51.6 us
  Pallas kernels  49 us (93%)
  local copies, waits for them, and re-layouts  2.53 us (5%)
    pallas_call x1, Pallas kernels, on_device(): pl.pallas_call(functools.partial(link_kernel, nd, nr), out_shape=jax.Shap...  24 us
    pallas_call x1, Pallas kernels, on_device(): pl.pallas_call(functools.partial(send_kernel, nd, nr), out_shape=jax.Shap...  22.4 us
    pallas_call x1, Pallas kernels, on_device(): pl.pallas_call(functools.partial(pack_kernel, nd), out_shape=jax.ShapeDty...  2.62 us
    unnamed x5, local copies, waits for them, and re-layouts  2.53 us

profile of v1, /device:TPU:1, one launch (start us, length us, event | category | flops | bytes accessed | tf_op | source)
XLA Modules:
  0.0 51.6 jit_solution(11541021661636033834)
XLA Ops:
  0.0 0.8 %copy.3.net_ref = s32[128,8]{1,0:T(8,128)S(1)} copy(s32[128,8]{0,1:T(8,128)} %param.3) | data formatting | bytes 8192 | tf_op args[1]
  0.8 2.6 %pack.1.s_ref = f32[2,2,8,72,128]{4,3,2,1,0:T(8,128)} custom-call(f32[2,64,8,256]{3,2,1,0:T(8,128)} %x_ref.1), custom_call_target="tpu_custom_call" | custom-call | tf_op jit(solution)/shard_map/pack/pallas_call | solution.py:340
  3.4 0.0 copy-start.1
  3.4 22.4 %send.1.e_ref = f32[2,2,18,72,128]{4,3,2,1,0:T(8,128)} custom-call(f32[2,2,8,72,128]{4,3,2,1,0:T(8,128)} %pack.1.s_ref), custom_call_target="tpu_custom_call" | custom-call | tf_op jit(solution)/shard_map/send/pallas_call | solution.py:348
  25.8 0.0 copy-done.1
  25.8 0.0 copy-start
  25.8 1.7 %copy-done = f32[2,2,18,72,128]{4,3,2,1,0:T(8,128)S(1)} copy-done((f32[2,2,18,72,128]{4,3,2,1,0:T(8,128)S(1)}, f32[2,2,18,72,128]{4,3,2,1,0:T(8,128)}, u32[]{:S(2)}) %copy-start) | copy-done | bytes 2654232
  27.6 24.0 %link.1 = f32[2,128,8,128]{3,2,1,0:T(8,128)} custom-call(f32[2,2,8,72,128]{4,3,2,1,0:T(8,128)S(1)} %copy-done.1, f32[2,2,18,72,128]{4,3,2,1,0:T(8,128)S(1)} %copy-done, s32[128,8]{1,0:T(8,128)S(1)} %copy.3.net_ref), custom_call_target="tpu_custom_call" | custom-call | tf_op jit(solution)/shard_map/link/pallas_call | solution.py:357
Async XLA Ops:
  3.4 22.4 %copy-start.1 = (f32[2,2,8,72,128]{4,3,2,1,0:T(8,128)S(1)}, f32[2,2,8,72,128]{4,3,2,1,0:T(8,128)}, u32[]{:S(2)}) copy-start(f32[2,2,8,72,128]{4,3,2,1,0:T(8,128)} %pack.1.s_ref) | copy-start | bytes 3538948
  25.8 1.8 %copy-start = (f32[2,2,18,72,128]{4,3,2,1,0:T(8,128)S(1)}, f32[2,2,18,72,128]{4,3,2,1,0:T(8,128)}, u32[]{:S(2)}) copy-start(f32[2,2,18,72,128]{4,3,2,1,0:T(8,128)} %send.1.e_ref) | copy-start | bytes 7962628

commit v2 on v1

--- a/solution.py
+++ b/solution.py
@@ -10,6 +10,7 @@
 LOOK = 5
 ITERS = 5
 SUB = 8
+STEP = 8
 MESH = pl.DeviceIdType.MESH
 
 
@@ -42,7 +43,10 @@
 
 
 def send_kernel(nd, nr, s_ref, e_ref, give_sem, take_sem, up_send, up_recv, down_send, down_recv):
-    rows = s_ref.shape[2]
+    rows, deep = s_ref.shape[2:4]
+    parts = give_sem.shape[1] // 2
+    piece = deep // parts
+    chunks = [(comp, part) for comp in range(2) for part in range(parts)]
     me = lax.axis_index("date")
     row = lax.axis_index("row")
     has_up = row > 0
@@ -63,65 +67,69 @@
 
     pl.semaphore_wait(barrier, nd - 1 + has_up.astype(jnp.int32) + has_down.astype(jnp.int32))
 
-    def give(k, comp):
+    def give(k, n):
+        comp, part = chunks[n]
         there = lax.rem(me + k, nd)
+        near = pl.ds(part * piece, piece)
         return pltpu.make_async_remote_copy(
-            src_ref=s_ref.at[there, comp],
-            dst_ref=e_ref.at[me, comp, pl.ds(LOOK, rows)],
-            send_sem=give_sem.at[k, comp],
-            recv_sem=take_sem.at[k, comp],
+            src_ref=s_ref.at[there, comp, :, near],
+            dst_ref=e_ref.at[me, comp, pl.ds(LOOK, rows), near],
+            send_sem=give_sem.at[k, n],
+            recv_sem=take_sem.at[k, n],
             device_id=(there, row),
             device_id_type=MESH,
         )
 
-    def rim(k, comp, to_up):
+    def rim(k, n, to_up):
+        comp, part = chunks[n]
+        near = pl.ds(part * piece, piece)
         source = lax.rem(me + nd - k, nd)
         begin = 0 if to_up else rows - LOOK
         if k == 0:
-            src = s_ref.at[me, comp, pl.ds(begin, LOOK)]
+            src = s_ref.at[me, comp, pl.ds(begin, LOOK), near]
         else:
-            src = e_ref.at[source, comp, pl.ds(LOOK + begin, LOOK)]
+            src = e_ref.at[source, comp, pl.ds(LOOK + begin, LOOK), near]
         return pltpu.make_async_remote_copy(
             src_ref=src,
-            dst_ref=e_ref.at[source, comp, pl.ds(LOOK + rows if to_up else 0, LOOK)],
-            send_sem=(up_send if to_up else down_send).at[k, comp],
-            recv_sem=(up_recv if to_up else down_recv).at[k, comp],
+            dst_ref=e_ref.at[source, comp, pl.ds(LOOK + rows if to_up else 0, LOOK), near],
+            send_sem=(up_send if to_up else down_send).at[k, n],
+            recv_sem=(up_recv if to_up else down_recv).at[k, n],
             device_id=(me, up if to_up else down),
             device_id_type=MESH,
         )
 
-    def start_rims(k, comp):
+    def start_rims(k, n):
         @pl.when(has_up)
         def _():
-            rim(k, comp, True).start()
+            rim(k, n, True).start()
 
         @pl.when(has_down)
         def _():
-            rim(k, comp, False).start()
-
-    for comp in range(2):
+            rim(k, n, False).start()
+
+    for n in range(len(chunks)):
         for k in range(1, nd):
-            give(k, comp).start()
-        start_rims(0, comp)
-    for comp in range(2):
+            give(k, n).start()
+        start_rims(0, n)
+    for n in range(len(chunks)):
         for k in range(1, nd):
-            give(k, comp).wait_recv()
-            start_rims(k, comp)
-    for comp in range(2):
+            give(k, n).wait_recv()
+            start_rims(k, n)
+    for n in range(len(chunks)):
         for k in range(1, nd):
-            give(k, comp).wait_send()
-    for comp in range(2):
+            give(k, n).wait_send()
+    for n in range(len(chunks)):
         for k in range(nd):
 
             @pl.when(has_up)
             def _():
-                rim(k, comp, True).wait_send()
-                rim(k, comp, False).wait_recv()
+                rim(k, n, True).wait_send()
+                rim(k, n, False).wait_recv()
 
             @pl.when(has_down)
             def _():
-                rim(k, comp, False).wait_send()
-                rim(k, comp, True).wait_recv()
+                rim(k, n, False).wait_send()
+                rim(k, n, True).wait_recv()
 
 
 def row_sums(cells):
@@ -174,10 +182,10 @@
         return self.read(comp, row, offset)
 
 
-def link_kernel(nd, nr, s_ref, e_ref, net_ref, out_ref, main, rim, rim_high, rim_low, table, root, gam, vec):
+def link_kernel(nd, nr, s_ref, e_ref, net_ref, out_ref, main, rim, rim_high, rim_low, table, root, gam, vec, used_at):
     rows, width = out_ref.shape[2], out_ref.shape[3]
     dates = out_ref.shape[1]
-    band = net_ref.shape[1]
+    band = net_ref.shape[0]
     local = dates // nd
     groups = local // SUB
     slot = width // groups
@@ -187,6 +195,8 @@
     row = lax.axis_index("row")
     has_up = row > 0
     has_down = row < nr - 1
+
+    used_at[...] = jnp.transpose(net_ref[...].astype(jnp.float32), (1, 0))
 
     lane = lax.broadcasted_iota(jnp.int32, (SUB, width), 1)
     for comp in range(2):
@@ -242,7 +252,7 @@
         s, g = t // groups, lax.rem(t, groups)
         base = t * SUB
         load = Loader(lambda comp, r, off: main[comp, r, pl.ds(base + off, SUB), :], tall)
-        used = net_ref[pl.ds(base, SUB), :].astype(jnp.float32)
+        used = used_at[pl.ds(base, SUB), :]
         begin = 0
         for offset in range(band + 1):
             high, low = halves(products(load, offset))
@@ -259,8 +269,11 @@
                     weight = root[k, pl.ds(base, SUB), :] * root[k, pl.ds(base + offset, SUB), :]
                     weight = weight * used[:, offset - 1 : offset]
                     at = pl.ds(base * rows + k, SUB, stride=rows)
-                    gam[0, offset - 1, at, :] = sums[k * SUB : (k + 1) * SUB] * weight
-                    gam[1, offset - 1, at, :] = sums[(rows + k) * SUB : (rows + k + 1) * SUB] * weight
+                    c_re = sums[k * SUB : (k + 1) * SUB] * weight
+                    c_im = sums[(rows + k) * SUB : (rows + k + 1) * SUB] * weight
+                    gam[0, offset - 1, at, :] = c_re
+                    gam[1, offset - 1, at, :] = c_re + c_im
+                    gam[2, offset - 1, at, :] = c_im - c_re
         return carry
 
     lax.fori_loop(0, tiles, tile_sums, 0)
@@ -271,12 +284,37 @@
             for d in range(band):
                 vec[buf, comp, dates + d] = zero
 
-    def fill(d, carry):
-        vec[0, 0, d] = zero + 1.0
-        vec[0, 1, d] = zero
-        return carry
-
-    lax.fori_loop(0, dates, fill, 0)
+    def at_date(d):
+        return pl.ds(pl.multiple_of(d * rows, rows), rows)
+
+    def first(b, carry):
+        back_re, back_sum, total = list(carry[0]), list(carry[1]), carry[2]
+        for j in range(SUB):
+            d = b * SUB + j
+            y_re = back_re[j] + 1.0
+            y_im = back_re[j] - back_sum[j]
+            ahead_re = ahead_sum = None
+            for o in range(1, band + 1):
+                c_re = gam[0, o - 1, at_date(d), :]
+                c_sum = gam[1, o - 1, at_date(d), :]
+                ahead_re = c_re if ahead_re is None else ahead_re + c_re
+                ahead_sum = c_sum if ahead_sum is None else ahead_sum + c_sum
+                if o == band:
+                    back_re.append(c_re)
+                    back_sum.append(c_sum)
+                else:
+                    back_re[j + o] = back_re[j + o] + c_re
+                    back_sum[j + o] = back_sum[j + o] + c_sum
+            y_re = y_re + ahead_re
+            y_im = y_im + (ahead_sum - ahead_re)
+            vec[1, 0, d] = y_re
+            vec[1, 1, d] = y_im
+            total = total + (y_re * y_re + y_im * y_im)
+        return tuple(back_re[SUB:]), tuple(back_sum[SUB:]), total
+
+    none = tuple(zero for _ in range(band))
+    _, _, total = lax.fori_loop(0, tiles, first, (none, none, zero))
+    scale = lax.rsqrt(total / dates + 1e-06)
 
     def iterate(step, scale):
         now = lax.rem(step, 2)
@@ -284,49 +322,58 @@
 
         def block(b, carry):
             acc, near, total = carry
-            acc_re, acc_im = [list(a) for a in acc]
-            v_re, v_im = [list(a) for a in near]
-            for j in range(SUB):
-                d = b * SUB + j
+            acc_a, acc_b, acc_c = [list(a) for a in acc]
+            v_re, v_im, v_sum = [list(a) for a in near]
+            for j in range(STEP):
+                d = b * STEP + j
                 v_re.append(vec[now, 0, d + band])
                 v_im.append(vec[now, 1, d + band])
-                y_re = acc_re[j] + v_re[j]
-                y_im = acc_im[j] + v_im[j]
-                at = pl.ds(pl.multiple_of(d * rows, rows), rows)
+                v_sum.append(v_re[-1] + v_im[-1])
+                y_a, y_b, y_c = acc_a[j], -acc_b[j], -acc_c[j]
                 for o in range(1, band + 1):
-                    c_re = gam[0, o - 1, at, :]
-                    c_im = gam[1, o - 1, at, :]
-                    y_re = y_re + (c_re * v_re[j + o] - c_im * v_im[j + o])
-                    y_im = y_im + (c_re * v_im[j + o] + c_im * v_re[j + o])
-                    back_re = c_re * v_re[j] + c_im * v_im[j]
-                    back_im = c_re * v_im[j] - c_im * v_re[j]
+                    c_re = gam[0, o - 1, at_date(d), :]
+                    c_sum = gam[1, o - 1, at_date(d), :]
+                    c_dif = gam[2, o - 1, at_date(d), :]
+                    y_a = y_a + c_re * v_sum[j + o]
+                    y_b = y_b + c_dif * v_re[j + o]
+                    y_c = y_c + c_sum * v_im[j + o]
+                    back_a = c_re * v_sum[j]
+                    back_b = c_sum * v_re[j]
+                    back_c = c_dif * v_im[j]
                     if o == band:
-                        acc_re.append(back_re)
-                        acc_im.append(back_im)
+                        acc_a.append(back_a)
+                        acc_b.append(back_b)
+                        acc_c.append(back_c)
                     else:
-                        acc_re[j + o] = acc_re[j + o] + back_re
-                        acc_im[j + o] = acc_im[j + o] + back_im
+                        acc_a[j + o] = acc_a[j + o] + back_a
+                        acc_b[j + o] = acc_b[j + o] + back_b
+                        acc_c[j + o] = acc_c[j + o] + back_c
+                y_re = v_re[j] + (y_a - y_c)
+                y_im = v_im[j] + (y_a + y_b)
                 vec[after, 0, d] = y_re
                 vec[after, 1, d] = y_im
                 total = total + (y_re * y_re + y_im * y_im)
-            acc = tuple(acc_re[SUB:]), tuple(acc_im[SUB:])
-            near = tuple(v_re[SUB:]), tuple(v_im[SUB:])
+            acc = tuple(acc_a[STEP:]), tuple(acc_b[STEP:]), tuple(acc_c[STEP:])
+            near = tuple(v_re[STEP:]), tuple(v_im[STEP:]), tuple(v_sum[STEP:])
             return acc, near, total
 
-        none = tuple(zero for _ in range(band))
-        near = tuple(tuple(vec[now, comp, d] for d in range(band)) for comp in range(2))
-        _, _, total = lax.fori_loop(0, tiles, block, ((none, none), near, zero))
+        v_re = tuple(vec[now, 0, d] for d in range(band))
+        v_im = tuple(vec[now, 1, d] for d in range(band))
+        v_sum = tuple(a + b for a, b in zip(v_re, v_im))
+        _, _, total = lax.fori_loop(0, dates // STEP, block, ((none, none, none), (v_re, v_im, v_sum), zero))
         return scale * lax.rsqrt(scale * scale * (total / dates) + 1e-06)
 
-    scale = lax.fori_loop(0, ITERS, iterate, zero + 1.0)
+    scale = lax.fori_loop(1, ITERS, iterate, scale)
     final = ITERS % 2
 
-    def finish(d, carry):
-        out_ref[0, d] = vec[final, 0, d] * scale
-        out_ref[1, d] = vec[final, 1, d] * scale
+    def finish(b, carry):
+        for j in range(SUB):
+            d = b * SUB + j
+            out_ref[0, d] = vec[final, 0, d] * scale
+            out_ref[1, d] = vec[final, 1, d] * scale
         return carry
 
-    lax.fori_loop(0, dates, finish, 0)
+    lax.fori_loop(0, tiles, finish, 0)
 
 
 def on_device(nd, nr, slc, network):
@@ -336,7 +383,6 @@
     tall = rows + 2 * LOOK
     maps = (2 * band + 1) * rows * SUB
     whole = pl.BlockSpec(memory_space=pltpu.VMEM)
-    away = pl.BlockSpec(memory_space=pl.ANY)
     packed = pl.pallas_call(
         functools.partial(pack_kernel, nd),
         out_shape=jax.ShapeDtypeStruct((nd, 2, rows, local + SUB, width), jnp.float32),
@@ -344,12 +390,13 @@
         out_specs=whole,
         name="pack",
     )(slc)
-    sems = pltpu.SemaphoreType.DMA((nd, 2))
+    parts = 3 if (local + SUB) % (3 * SUB) == 0 else 1
+    sems = pltpu.SemaphoreType.DMA((nd, 2 * parts))
     landed = pl.pallas_call(
         functools.partial(send_kernel, nd, nr),
         out_shape=jax.ShapeDtypeStruct((nd, 2, tall, local + SUB, width), jnp.float32),
-        in_specs=[away],
-        out_specs=away,
+        in_specs=[whole],
+        out_specs=whole,
         scratch_shapes=[sems] * 6,
         compiler_params=pltpu.CompilerParams(collective_id=0, has_side_effects=True),
         name="send",
@@ -366,12 +413,13 @@
             pltpu.VMEM((nd, maps, width), jnp.bfloat16),
             pltpu.VMEM((local // SUB, 2 * width, width), jnp.bfloat16),
             pltpu.VMEM((rows, dates + SUB, width), jnp.float32),
-            pltpu.VMEM((2, band, dates * rows, width), jnp.float32),
+            pltpu.VMEM((3, band, dates * rows, width), jnp.float32),
             pltpu.VMEM((2, 2, dates + band, rows, width), jnp.float32),
+            pltpu.VMEM((dates, band), jnp.float32),
         ],
         compiler_params=pltpu.CompilerParams(vmem_limit_bytes=48 * 1024 * 1024),
         name="link",
-    )(packed, landed, network)
+    )(packed, landed, network.T)
 
 
 def solution(mesh):

time: 52.6 us -> 48.7 us (0.926); the launches traced: 51.6 us -> 48.5 us
  Pallas kernels: 49 us -> 46.7 us
  local copies, waits for them, and re-layouts: 2.53 us -> 1.75 us
    pallas_call x1, Pallas kernels: 24 us -> 20.3 us  [on_device(): pl.pallas_call(functools.partial(link_kernel, nd, nr), out_shape=jax.Shap...]
    pallas_call x1, Pallas kernels: 22.4 us -> 23.7 us  [on_device(): pl.pallas_call(functools.partial(send_kernel, nd, nr), out_shape=jax.Shap...]
    unnamed x5 -> x6, local copies, waits for them, and re-layouts: 2.53 us -> 1.75 us
where the time goes in v2:
time: 48.7 us; the launch traced here: 48.5 us
  Pallas kernels  46.7 us (96%)
  local copies, waits for them, and re-layouts  1.75 us (4%)
    pallas_call x1, Pallas kernels, on_device(): pl.pallas_call(functools.partial(send_kernel, nd, nr), out_shape=jax.Shap...  23.7 us
    pallas_call x1, Pallas kernels, on_device(): pl.pallas_call(functools.partial(link_kernel, nd, nr), out_shape=jax.Shap...  20.3 us
    pallas_call x1, Pallas kernels, on_device(): pl.pallas_call(functools.partial(pack_kernel, nd), out_shape=jax.ShapeDty...  2.63 us
    unnamed x6, local copies, waits for them, and re-layouts  1.75 us

profile of v2, /device:TPU:1, one launch (start us, length us, event | category | flops | bytes accessed | tf_op | source)
XLA Modules:
  0.0 48.5 jit_solution(14161955140717733256)
XLA Ops:
  0.0 0.0 copy-start.2
  0.0 2.6 %pack.1.s_ref = f32[2,2,8,72,128]{4,3,2,1,0:T(8,128)} custom-call(f32[2,64,8,256]{3,2,1,0:T(8,128)} %x_ref.1), custom_call_target="tpu_custom_call" | custom-call | tf_op jit(solution)/shard_map/pack/pallas_call | solution.py:386
  2.6 0.0 copy-start.1
  2.6 23.7 %send.1.e_ref = f32[2,2,18,72,128]{4,3,2,1,0:T(8,128)} custom-call(f32[2,2,8,72,128]{4,3,2,1,0:T(8,128)} %pack.1.s_ref), custom_call_target="tpu_custom_call" | custom-call | tf_op jit(solution)/shard_map/send/pallas_call | solution.py:395
  26.4 0.0 copy-done.2
  26.4 0.0 copy-done.1
  26.4 0.0 copy-start
  26.4 1.7 %copy-done = f32[2,2,18,72,128]{4,3,2,1,0:T(8,128)S(1)} copy-done((f32[2,2,18,72,128]{4,3,2,1,0:T(8,128)S(1)}, f32[2,2,18,72,128]{4,3,2,1,0:T(8,128)}, u32[]{:S(2)}) %copy-start) | copy-done | bytes 2654232
  28.2 20.3 %link.1 = f32[2,128,8,128]{3,2,1,0:T(8,128)} custom-call(f32[2,2,8,72,128]{4,3,2,1,0:T(8,128)S(1)} %copy-done.1, f32[2,2,18,72,128]{4,3,2,1,0:T(8,128)S(1)} %copy-done, s32[8,128]{1,0:T(8,128)S(1)} %bitcast.1), custom_call_target="tpu_custom_call" | custom-call | tf_op jit(solution)/shard_map/link/pallas_call | solution.py:404
Async XLA Ops:
  0.0 26.4 %copy-start.2 = (s32[128,8]{0,1:T(8,128)S(1)}, s32[128,8]{0,1:T(8,128)}, u32[]{:S(2)}) copy-start(s32[128,8]{0,1:T(8,128)} %param.3) | copy-start | bytes 12292
  2.6 23.8 %copy-start.1 = (f32[2,2,8,72,128]{4,3,2,1,0:T(8,128)S(1)}, f32[2,2,8,72,128]{4,3,2,1,0:T(8,128)}, u32[]{:S(2)}) copy-start(f32[2,2,8,72,128]{4,3,2,1,0:T(8,128)} %pack.1.s_ref) | copy-start | bytes 3538948
  26.4 1.8 %copy-start = (f32[2,2,18,72,128]{4,3,2,1,0:T(8,128)S(1)}, f32[2,2,18,72,128]{4,3,2,1,0:T(8,128)}, u32[]{:S(2)}) copy-start(f32[2,2,18,72,128]{4,3,2,1,0:T(8,128)} %send.1.e_ref) | copy-start | bytes 7962628

commit v3 on v2

--- a/solution.py
+++ b/solution.py
@@ -10,7 +10,7 @@
 LOOK = 5
 ITERS = 5
 SUB = 8
-STEP = 8
+STEP = 16
 MESH = pl.DeviceIdType.MESH
 
 
@@ -383,6 +383,7 @@
     tall = rows + 2 * LOOK
     maps = (2 * band + 1) * rows * SUB
     whole = pl.BlockSpec(memory_space=pltpu.VMEM)
+    away = pl.BlockSpec(memory_space=pl.ANY)
     packed = pl.pallas_call(
         functools.partial(pack_kernel, nd),
         out_shape=jax.ShapeDtypeStruct((nd, 2, rows, local + SUB, width), jnp.float32),
@@ -395,8 +396,8 @@
     landed = pl.pallas_call(
         functools.partial(send_kernel, nd, nr),
         out_shape=jax.ShapeDtypeStruct((nd, 2, tall, local + SUB, width), jnp.float32),
-        in_specs=[whole],
-        out_specs=whole,
+        in_specs=[away],
+        out_specs=away,
         scratch_shapes=[sems] * 6,
         compiler_params=pltpu.CompilerParams(collective_id=0, has_side_effects=True),
         name="send",

time: 48.7 us -> 45.8 us (0.940)
  Pallas kernels: 46.7 us -> 43.9 us
    pallas_call x1, Pallas kernels: 23.7 us -> 21.5 us  [on_device(): pl.pallas_call(functools.partial(send_kernel, nd, nr), out_shape=jax.Shap...]
    pallas_call x1, Pallas kernels: 20.3 us -> 19.8 us  [on_device(): pl.pallas_call(functools.partial(link_kernel, nd, nr), out_shape=jax.Shap...]
where the time goes in v3:
time: 45.8 us; the launch traced here: 45.7 us
  Pallas kernels  43.9 us (96%)
  local copies, waits for them, and re-layouts  1.75 us (4%)
    pallas_call x1, Pallas kernels, on_device(): pl.pallas_call(functools.partial(send_kernel, nd, nr), out_shape=jax.Shap...  21.5 us
    pallas_call x1, Pallas kernels, on_device(): pl.pallas_call(functools.partial(link_kernel, nd, nr), out_shape=jax.Shap...  19.8 us
    pallas_call x1, Pallas kernels, on_device(): pl.pallas_call(functools.partial(pack_kernel, nd), out_shape=jax.ShapeDty...  2.63 us
    unnamed x6, local copies, waits for them, and re-layouts  1.75 us

profile of v3, /device:TPU:1, one launch (start us, length us, event | category | flops | bytes accessed | tf_op | source)
XLA Modules:
  0.0 45.7 jit_solution(5872668122116504957)
XLA Ops:
  0.0 0.0 copy-start.2
  0.0 2.6 %pack.1.s_ref = f32[2,2,8,72,128]{4,3,2,1,0:T(8,128)} custom-call(f32[2,64,8,256]{3,2,1,0:T(8,128)} %x_ref.1), custom_call_target="tpu_custom_call" | custom-call | tf_op jit(solution)/shard_map/pack/pallas_call | solution.py:387
  2.6 0.0 copy-start.1
  2.6 21.5 %send.1.e_ref = f32[2,2,18,72,128]{4,3,2,1,0:T(8,128)} custom-call(f32[2,2,8,72,128]{4,3,2,1,0:T(8,128)} %pack.1.s_ref), custom_call_target="tpu_custom_call" | custom-call | tf_op jit(solution)/shard_map/send/pallas_call | solution.py:396
  24.1 0.0 copy-done.2
  24.2 0.0 copy-done.1
  24.2 0.0 copy-start
  24.2 1.7 %copy-done = f32[2,2,18,72,128]{4,3,2,1,0:T(8,128)S(1)} copy-done((f32[2,2,18,72,128]{4,3,2,1,0:T(8,128)S(1)}, f32[2,2,18,72,128]{4,3,2,1,0:T(8,128)}, u32[]{:S(2)}) %copy-start) | copy-done | bytes 2654232
  25.9 19.8 %link.1 = f32[2,128,8,128]{3,2,1,0:T(8,128)} custom-call(f32[2,2,8,72,128]{4,3,2,1,0:T(8,128)S(1)} %copy-done.1, f32[2,2,18,72,128]{4,3,2,1,0:T(8,128)S(1)} %copy-done, s32[8,128]{1,0:T(8,128)S(1)} %bitcast.1), custom_call_target="tpu_custom_call" | custom-call | tf_op jit(solution)/shard_map/link/pallas_call | solution.py:405
Async XLA Ops:
  0.0 24.1 %copy-start.2 = (s32[128,8]{0,1:T(8,128)S(1)}, s32[128,8]{0,1:T(8,128)}, u32[]{:S(2)}) copy-start(s32[128,8]{0,1:T(8,128)} %param.3) | copy-start | bytes 12292
  2.6 21.5 %copy-start.1 = (f32[2,2,8,72,128]{4,3,2,1,0:T(8,128)S(1)}, f32[2,2,8,72,128]{4,3,2,1,0:T(8,128)}, u32[]{:S(2)}) copy-start(f32[2,2,8,72,128]{4,3,2,1,0:T(8,128)} %pack.1.s_ref) | copy-start | bytes 3538948
  24.2 1.8 %copy-start = (f32[2,2,18,72,128]{4,3,2,1,0:T(8,128)S(1)}, f32[2,2,18,72,128]{4,3,2,1,0:T(8,128)}, u32[]{:S(2)}) copy-start(f32[2,2,18,72,128]{4,3,2,1,0:T(8,128)} %send.1.e_ref) | copy-start | bytes 7962628

commit v4 on v3

--- a/solution.py
+++ b/solution.py
@@ -260,8 +260,8 @@
             high = jnp.concatenate([high, rim_high[s, pl.ds(begin, count), :]], axis=1)
             low = jnp.concatenate([low, rim_low[s, pl.ds(begin, count), :]], axis=1)
             begin += count
-            sums = jnp.dot(jnp.concatenate([high, low], axis=0), table[g], preferred_element_type=jnp.float32)
-            sums = sums[:count] + sums[count:]
+            sums = jnp.dot(high, table[g], preferred_element_type=jnp.float32)
+            sums = sums + jnp.dot(low, table[g], preferred_element_type=jnp.float32)
             for k in range(rows):
                 if offset == 0:
                     root[k, pl.ds(base, SUB), :] = lax.rsqrt(sums[k * SUB : (k + 1) * SUB] + 1e-06)
@@ -391,7 +391,7 @@
         out_specs=whole,
         name="pack",
     )(slc)
-    parts = 3 if (local + SUB) % (3 * SUB) == 0 else 1
+    parts = (local + SUB) // SUB
     sems = pltpu.SemaphoreType.DMA((nd, 2 * parts))
     landed = pl.pallas_call(
         functools.partial(send_kernel, nd, nr),

time: 45.8 us -> 46.7 us (1.020)
  Pallas kernels: 43.9 us -> 44.8 us
    pallas_call x1, Pallas kernels: 21.5 us -> 22.3 us  [on_device(): pl.pallas_call(functools.partial(send_kernel, nd, nr), out_shape=jax.Shap...]
where the time goes in v4:
time: 46.7 us; the launch traced here: 46.6 us
  Pallas kernels  44.8 us (96%)
  local copies, waits for them, and re-layouts  1.75 us (4%)
    pallas_call x1, Pallas kernels, on_device(): pl.pallas_call(functools.partial(send_kernel, nd, nr), out_shape=jax.Shap...  22.3 us
    pallas_call x1, Pallas kernels, on_device(): pl.pallas_call(functools.partial(link_kernel, nd, nr), out_shape=jax.Shap...  19.8 us
    pallas_call x1, Pallas kernels, on_device(): pl.pallas_call(functools.partial(pack_kernel, nd), out_shape=jax.ShapeDty...  2.63 us
    unnamed x6, local copies, waits for them, and re-layouts  1.75 us

profile of v4, /device:TPU:1, one launch (start us, length us, event | category | flops | bytes accessed | tf_op | source)
XLA Modules:
  0.0 46.6 jit_solution(1874610077234484360)
XLA Ops:
  0.0 0.0 copy-start.2
  0.0 2.6 %pack.1.s_ref = f32[2,2,8,72,128]{4,3,2,1,0:T(8,128)} custom-call(f32[2,64,8,256]{3,2,1,0:T(8,128)} %x_ref.1), custom_call_target="tpu_custom_call" | custom-call | tf_op jit(solution)/shard_map/pack/pallas_call | solution.py:387
  2.6 0.0 copy-start.1
  2.6 22.3 %send.1.e_ref = f32[2,2,18,72,128]{4,3,2,1,0:T(8,128)} custom-call(f32[2,2,8,72,128]{4,3,2,1,0:T(8,128)} %pack.1.s_ref), custom_call_target="tpu_custom_call" | custom-call | tf_op jit(solution)/shard_map/send/pallas_call | solution.py:396
  25.0 0.0 copy-done.2
  25.0 0.0 copy-done.1
  25.0 0.0 copy-start
  25.0 1.7 %copy-done = f32[2,2,18,72,128]{4,3,2,1,0:T(8,128)S(1)} copy-done((f32[2,2,18,72,128]{4,3,2,1,0:T(8,128)S(1)}, f32[2,2,18,72,128]{4,3,2,1,0:T(8,128)}, u32[]{:S(2)}) %copy-start) | copy-done | bytes 2654232
  26.8 19.8 %link.1 = f32[2,128,8,128]{3,2,1,0:T(8,128)} custom-call(f32[2,2,8,72,128]{4,3,2,1,0:T(8,128)S(1)} %copy-done.1, f32[2,2,18,72,128]{4,3,2,1,0:T(8,128)S(1)} %copy-done, s32[8,128]{1,0:T(8,128)S(1)} %bitcast.1), custom_call_target="tpu_custom_call" | custom-call | tf_op jit(solution)/shard_map/link/pallas_call | solution.py:405
Async XLA Ops:
  0.0 25.0 %copy-start.2 = (s32[128,8]{0,1:T(8,128)S(1)}, s32[128,8]{0,1:T(8,128)}, u32[]{:S(2)}) copy-start(s32[128,8]{0,1:T(8,128)} %param.3) | copy-start | bytes 12292
  2.6 22.4 %copy-start.1 = (f32[2,2,8,72,128]{4,3,2,1,0:T(8,128)S(1)}, f32[2,2,8,72,128]{4,3,2,1,0:T(8,128)}, u32[]{:S(2)}) copy-start(f32[2,2,8,72,128]{4,3,2,1,0:T(8,128)} %pack.1.s_ref) | copy-start | bytes 3538948
  25.0 1.8 %copy-start = (f32[2,2,18,72,128]{4,3,2,1,0:T(8,128)S(1)}, f32[2,2,18,72,128]{4,3,2,1,0:T(8,128)}, u32[]{:S(2)}) copy-start(f32[2,2,18,72,128]{4,3,2,1,0:T(8,128)} %send.1.e_ref) | copy-start | bytes 7962628
